TPU v7x, 128 devices: a whole 4x4x4 slice. The times are simulated.
128 devices in a mesh: vox: 8 (over y, core), fas: 16 (over z, x).
Axes of the slice: x: 4, y: 4, z: 4, core: 2. Of those that a mesh axis runs over, the one named last changes fastest.
Arguments:
- signal: float32 [128, 6144], P('vox', 'fas'), may hold values from -6 to 6
- initial_weights: float32 [524288], P('fas'), may hold values from 0.1 to 2
- coefficients: bfloat16 [32768, 4096], P(('vox', 'fas')), may hold values from 0 to 0.0234375
- block_rows: int32 [32768], P(('vox', 'fas')), may hold values from 0 to 127, as said below
- block_cols: int32 [32768], P(('vox', 'fas')), may hold values from 0 to 8191, as said below
- block_atoms: int32 [32768, 64], P(('vox', 'fas')), may hold values from 0 to 359
- block_count: int32 [128], P(('vox', 'fas')), may hold values from 64 to 256, as said below
- dictionary: bfloat16 [360, 96], replicated, may hold values from -6 to 6
Outputs:
- weights: float32 [524288], P('fas')
- residual: float32 [128, 6144], P('vox', 'fas')
Inputs may be any that keep to these rules, and one draw needn't show every extreme that they name: Block slots are stored device by device: the device with vox index i and fas index f holds slots (i * 16 + f) * 256 to (i * 16 + f + 1) * 256 - 1, and every block_rows value there lies in i * 16 to (i + 1) * 16 - 1. For the slots of the device with fas index f, every block_cols value lies in f * 512 to (f + 1) * 512 - 1. `block_count`: entry i * 16 + f is the number of live slots of the device with vox index i and fas index f, its first slots; some device has all 256 live.
All inputs are finite; a program needn't handle non-finite values.
Results may differ from a plain program's by a relative error of at most 0.0003.
Values sent between devices are 32-bit elements; how exact they have to be, the bound alone decides.
A program may use at most 128 MiB of HBM per device.

v0:
```python
import jax
import jax.numpy as jnp
from jax import lax
from jax.sharding import PartitionSpec as P

BV = 64
BF = 64
DIRS = 96
ITERS = 5


def local(
    signal,
    initial_weights,
    coefficients,
    block_rows,
    block_cols,
    block_atoms,
    block_count,
    dictionary,
):
    vox_rows = signal.shape[0]
    fas_rows = initial_weights.shape[0] // BF
    slot_total = coefficients.shape[0]
    row_width = BV * DIRS
    fas_place = lax.axis_index("fas")
    rows_local = block_rows - lax.axis_index("vox") * vox_rows
    cols_local = block_cols - fas_place * fas_rows
    live_count = block_count[0]
    atom_table = dictionary[block_atoms]
    coef_view = coefficients.reshape(slot_total, BV, BF)
    group_size = min(256, slot_total)
    group_turns = (live_count + group_size - 1) // group_size
    vox_range = jnp.arange(vox_rows, dtype=jnp.int32)
    fas_range = jnp.arange(fas_rows, dtype=jnp.int32)

    def group_pieces(first_slot):
        live_mask = (first_slot + jnp.arange(group_size, dtype=jnp.int32) < live_count).astype(
            jnp.float32
        )
        return (coef_view, atom_table, rows_local, cols_local, live_mask)

    def forward_partial(values):
        table = values.reshape(fas_rows, BF)

        def forward_accumulate(turn, running):
            coef_blk, atom_blk, rows_blk, cols_blk, live_mask = group_pieces(turn * group_size)
            scaled = coef_blk.astype(jnp.float32) * table[cols_blk][:, None, :]
            image_blk = jnp.einsum(
                "kvj,kjd->kvd",
                scaled,
                atom_blk.astype(jnp.float32),
                precision=lax.Precision.HIGHEST,
                preferred_element_type=jnp.float32,
            )
            selector = (rows_blk[:, None] == vox_range[None, :]).astype(jnp.float32) * live_mask[
                :, None
            ]
            added = jnp.dot(
                selector.T,
                image_blk.reshape(group_size, row_width),
                precision=lax.Precision.HIGHEST,
                preferred_element_type=jnp.float32,
            )
            return running + added

        start = jnp.zeros((vox_rows, row_width), jnp.float32)
        return lax.fori_loop(0, group_turns, forward_accumulate, start)

    def backward_partial(rows_view):

        def backward_accumulate(turn, running):
            coef_blk, atom_blk, rows_blk, cols_blk, live_mask = group_pieces(turn * group_size)
            gathered = rows_view[rows_blk]
            inner = jnp.einsum(
                "kvj,kvd->kjd",
                coef_blk.astype(jnp.float32),
                gathered,
                precision=lax.Precision.HIGHEST,
                preferred_element_type=jnp.float32,
            )
            contrib = jnp.sum(atom_blk.astype(jnp.float32) * inner, axis=-1)
            selector = (cols_blk[:, None] == fas_range[None, :]).astype(jnp.float32) * live_mask[
                :, None
            ]
            added = jnp.dot(
                selector.T,
                contrib,
                precision=lax.Precision.HIGHEST,
                preferred_element_type=jnp.float32,
            )
            return running + added

        start = jnp.zeros((fas_rows, BF), jnp.float32)
        running = lax.fori_loop(0, group_turns, backward_accumulate, start)
        return running.reshape(-1)

    def collect(partial_value):
        return lax.psum_scatter(partial_value, "fas", scatter_dimension=1, tiled=True)

    weights = initial_weights
    residual = collect(forward_partial(weights)) - signal
    for sweep in range(ITERS):
        whole_rows = lax.all_gather(residual, "fas", axis=1, tiled=True)
        gradient = lax.psum(backward_partial(whole_rows.reshape(vox_rows, BV, DIRS)), "vox")
        projected = jnp.where((weights > 0) | (gradient < 0), gradient, 0.0)
        image_pred = collect(forward_partial(projected))
        image_local = jnp.sum(image_pred * image_pred)
        grad_sq = lax.psum(jnp.sum(projected * projected), "fas")
        image_sq = lax.psum(image_local, ("vox", "fas"))
        step_size = grad_sq / (image_sq + 1e-06)
        weights = jnp.maximum(weights - step_size * projected, 0.0)
        residual = collect(forward_partial(weights)) - signal
    return (weights, residual)


def solution(mesh):
    placed = (
        P("vox", "fas"),
        P("fas"),
        P(("vox", "fas"), None),
        P(("vox", "fas")),
        P(("vox", "fas")),
        P(("vox", "fas"), None),
        P(("vox", "fas")),
        P(),
    )
    return jax.shard_map(
        local, mesh=mesh, in_specs=placed, out_specs=(P("fas"), P("vox", "fas")), check_vma=False
    )
```

profile of v0, /device:TPU:0, one launch (start us, length us, event | category | flops | bytes accessed | tf_op | source)
XLA Modules:
  0.0 2227.8 jit_solution(15539309578874618926)
XLA Ops:
  18.6 57.4 %gather_fusion = bf16[16384,96]{1,0:T(8,128)(2,1)} fusion(bf16[360,96]{1,0:T(8,128)(2,1)S(1)} %copy.28, s32[16384]{0:T(1024)S(1)} %broadcast_clamp_fusion), kind=kCustom, calls=%fused_computation | custom fusion | bytes 6356992 | tf_op jit(solution)/shard_map/gather | solution.py:30
  76.7 27.9 %while.208 = (s32[]{:T(128)}, f32[16,6144]{1,0:T(8,128)S(1)}, s32[]{:T(128)}, s32[256]{0:T(256)S(1)}, s32[]{:T(128)}, /*index=5*/bf16[256,64,64]{2,1,0:T(8,128)(...) while((s32[]{:T(128)}, f32[16,6144]{1,0:T(8,128)S(1)}, ...), condition=%wide.region_1.2_spmd.clone, body=%wide.region_0.1_spmd.clone.sunk | while | flops 1512153856 | bytes 31263864 | solution.py:68
  105.5 74.3 %reduce-scatter.12.cloned.1.call-done = f32[16,384]{1,0:T(8,128)} async-done(((f32[16,6144]{1,0:T(8,128)}), f32[16,384]{1,0:T(8,128)}) %reduce-scatter.12.cloned.1.call-update) | async-done | bytes 24592 | tf_op jit(solution)/shard_map/reduce_scatter | solution.py:99
  180.5 23.5 %all_gather.15 = f32[16,6144]{1,0:T(8,128)S(1)} all-gather(f32[16,384]{1,0:T(8,128)S(1)} %sub.58), channel_id=1, replica_groups=mesh['vox'=8,'fas'=16] {'fas'}, dimensions={1}, use_global_device_ids=true | all-gather | bytes 417792 | tf_op jit(solution)/shard_map/all_gather | solution.py:104
  208.6 13.4 fusion.156
  224.2 58.0 %all-reduce.6.cloned.1.call-done = f32[32768]{0:T(1024)} async-done(((f32[32768]{0:T(1024)}), f32[32768]{0:T(1024)}) %all-reduce.6.cloned.1.call-update) | async-done | bytes 131088 | tf_op jit(solution)/shard_map/psum | solution.py:105
  284.7 28.3 %while.210 = (s32[]{:T(128)}, f32[16,6144]{1,0:T(8,128)S(1)}, s32[]{:T(128)}, s32[256]{0:T(256)S(1)}, s32[]{:T(128)}, /*index=5*/bf16[256,64,64]{2,1,0:T(8,128)(...) while((s32[]{:T(128)}, f32[16,6144]{1,0:T(8,128)S(1)}, ...), condition=%wide.region_10.11_spmd.clone, body=%wide.region_9.10_spmd.clone.sunk | while | flops 1512153856 | bytes 31263864 | solution.py:68
  313.8 70.8 %reduce-scatter.14.cloned.1.call-done = f32[16,384]{1,0:T(8,128)} async-done(((f32[16,6144]{1,0:T(8,128)}), f32[16,384]{1,0:T(8,128)}) %reduce-scatter.14.cloned.1.call-update) | async-done | bytes 24592 | tf_op jit(solution)/shard_map/reduce_scatter | solution.py:99
  386.1 38.8 %psum.106 = f32[]{:T(128)} all-reduce(f32[]{:T(128)} %get-tuple-element.2460), channel_id=1, replica_groups=mesh['vox'=8,'fas'=16] {'fas'}, use_global_device_ids=true, to_apply=%region_8.9 | all-reduce | flops 1 | bytes 8 | tf_op jit(solution)/shard_map/psum | solution.py:109
  424.8 62.7 %psum.107 = f32[]{:T(128)} all-reduce(f32[]{:T(128)} %multiply_reduce_fusion.9), channel_id=1, replica_groups=mesh['vox'=8,'fas'=16] {'vox','fas'}, use_global_device_ids=true, to_apply=%region_13.14 | all-reduce | flops 1 | bytes 8 | tf_op jit(solution)/shard_map/psum | solution.py:110
  489.8 28.1 %while.211 = (s32[]{:T(128)}, f32[16,6144]{1,0:T(8,128)S(1)}, s32[]{:T(128)}, s32[256]{0:T(256)S(1)}, s32[]{:T(128)}, /*index=5*/bf16[256,64,64]{2,1,0:T(8,128)(...) while((s32[]{:T(128)}, f32[16,6144]{1,0:T(8,128)S(1)}, ...), condition=%wide.region_15.16_spmd.clone, body=%wide.region_14.15_spmd.clone.sunk | while | flops 1512153856 | bytes 31263864 | solution.py:68
  518.7 69.0 %reduce-scatter.16.cloned.1.call-done = f32[16,384]{1,0:T(8,128)} async-done(((f32[16,6144]{1,0:T(8,128)}), f32[16,384]{1,0:T(8,128)}) %reduce-scatter.16.cloned.1.call-update) | async-done | bytes 24592 | tf_op jit(solution)/shard_map/reduce_scatter | solution.py:99
  588.5 23.5 %all_gather.16 = f32[16,6144]{1,0:T(8,128)S(1)} all-gather(f32[16,384]{1,0:T(8,128)S(1)} %sub.60), channel_id=1, replica_groups=mesh['vox'=8,'fas'=16] {'fas'}, dimensions={1}, use_global_device_ids=true | all-gather | bytes 417792 | tf_op jit(solution)/shard_map/all_gather | solution.py:104
  616.6 13.4 fusion.157
  632.2 58.0 %all-reduce.8.cloned.1.call-done = f32[32768]{0:T(1024)} async-done(((f32[32768]{0:T(1024)}), f32[32768]{0:T(1024)}) %all-reduce.8.cloned.1.call-update) | async-done | bytes 131088 | tf_op jit(solution)/shard_map/psum | solution.py:105
  692.7 28.2 %while.213 = (s32[]{:T(128)}, f32[16,6144]{1,0:T(8,128)S(1)}, s32[]{:T(128)}, s32[256]{0:T(256)S(1)}, s32[]{:T(128)}, /*index=5*/bf16[256,64,64]{2,1,0:T(8,128)(...) while((s32[]{:T(128)}, f32[16,6144]{1,0:T(8,128)S(1)}, ...), condition=%wide.region_24.25_spmd.clone, body=%wide.region_23.24_spmd.clone.sunk | while | flops 1512153856 | bytes 31263864 | solution.py:68
  721.7 70.8 %reduce-scatter.18.cloned.1.call-done = f32[16,384]{1,0:T(8,128)} async-done(((f32[16,6144]{1,0:T(8,128)}), f32[16,384]{1,0:T(8,128)}) %reduce-scatter.18.cloned.1.call-update) | async-done | bytes 24592 | tf_op jit(solution)/shard_map/reduce_scatter | solution.py:99
  793.8 38.8 %psum.109 = f32[]{:T(128)} all-reduce(f32[]{:T(128)} %get-tuple-element.2458), channel_id=1, replica_groups=mesh['vox'=8,'fas'=16] {'fas'}, use_global_device_ids=true, to_apply=%region_22.23 | all-reduce | flops 1 | bytes 8 | tf_op jit(solution)/shard_map/psum | solution.py:109
  832.6 62.8 %psum.110 = f32[]{:T(128)} all-reduce(f32[]{:T(128)} %multiply_reduce_fusion.8), channel_id=1, replica_groups=mesh['vox'=8,'fas'=16] {'vox','fas'}, use_global_device_ids=true, to_apply=%region_27.28 | all-reduce | flops 1 | bytes 8 | tf_op jit(solution)/shard_map/psum | solution.py:110
  897.6 28.4 %while.214 = (s32[]{:T(128)}, f32[16,6144]{1,0:T(8,128)S(1)}, s32[]{:T(128)}, s32[256]{0:T(256)S(1)}, s32[]{:T(128)}, /*index=5*/bf16[256,64,64]{2,1,0:T(8,128)(...) while((s32[]{:T(128)}, f32[16,6144]{1,0:T(8,128)S(1)}, ...), condition=%wide.region_29.30_spmd.clone, body=%wide.region_28.29_spmd.clone.sunk | while | flops 1512153856 | bytes 31263864 | solution.py:68
  926.8 69.0 %reduce-scatter.20.cloned.1.call-done = f32[16,384]{1,0:T(8,128)} async-done(((f32[16,6144]{1,0:T(8,128)}), f32[16,384]{1,0:T(8,128)}) %reduce-scatter.20.cloned.1.call-update) | async-done | bytes 24592 | tf_op jit(solution)/shard_map/reduce_scatter | solution.py:99
  996.6 23.5 %all_gather.17 = f32[16,6144]{1,0:T(8,128)S(1)} all-gather(f32[16,384]{1,0:T(8,128)S(1)} %sub.62), channel_id=1, replica_groups=mesh['vox'=8,'fas'=16] {'fas'}, dimensions={1}, use_global_device_ids=true | all-gather | bytes 417792 | tf_op jit(solution)/shard_map/all_gather | solution.py:104
  1024.6 13.4 fusion.158
  1040.3 58.0 %all-reduce.10.cloned.1.call-done = f32[32768]{0:T(1024)} async-done(((f32[32768]{0:T(1024)}), f32[32768]{0:T(1024)}) %all-reduce.10.cloned.1.call-update) | async-done | bytes 131088 | tf_op jit(solution)/shard_map/psum | solution.py:105
  1100.7 28.1 %while.216 = (s32[]{:T(128)}, f32[16,6144]{1,0:T(8,128)S(1)}, s32[]{:T(128)}, s32[256]{0:T(256)S(1)}, s32[]{:T(128)}, /*index=5*/bf16[256,64,64]{2,1,0:T(8,128)(...) while((s32[]{:T(128)}, f32[16,6144]{1,0:T(8,128)S(1)}, ...), condition=%wide.region_38.39_spmd.clone, body=%wide.region_37.38_spmd.clone.sunk | while | flops 1512153856 | bytes 31263864 | solution.py:68
  1129.6 70.8 %reduce-scatter.22.cloned.1.call-done = f32[16,384]{1,0:T(8,128)} async-done(((f32[16,6144]{1,0:T(8,128)}), f32[16,384]{1,0:T(8,128)}) %reduce-scatter.22.cloned.1.call-update) | async-done | bytes 24592 | tf_op jit(solution)/shard_map/reduce_scatter | solution.py:99
  1201.9 38.8 %psum.112 = f32[]{:T(128)} all-reduce(f32[]{:T(128)} %get-tuple-element.2456), channel_id=1, replica_groups=mesh['vox'=8,'fas'=16] {'fas'}, use_global_device_ids=true, to_apply=%region_36.37 | all-reduce | flops 1 | bytes 8 | tf_op jit(solution)/shard_map/psum | solution.py:109
  1240.6 62.7 %psum.113 = f32[]{:T(128)} all-reduce(f32[]{:T(128)} %multiply_reduce_fusion.7), channel_id=1, replica_groups=mesh['vox'=8,'fas'=16] {'vox','fas'}, use_global_device_ids=true, to_apply=%region_41.42 | all-reduce | flops 1 | bytes 8 | tf_op jit(solution)/shard_map/psum | solution.py:110
  1305.6 28.3 %while.217 = (s32[]{:T(128)}, f32[16,6144]{1,0:T(8,128)S(1)}, s32[]{:T(128)}, s32[256]{0:T(256)S(1)}, s32[]{:T(128)}, /*index=5*/bf16[256,64,64]{2,1,0:T(8,128)(...) while((s32[]{:T(128)}, f32[16,6144]{1,0:T(8,128)S(1)}, ...), condition=%wide.region_43.44_spmd.clone, body=%wide.region_42.43_spmd.clone.sunk | while | flops 1512153856 | bytes 31263864 | solution.py:68
  1334.7 69.1 %reduce-scatter.24.cloned.1.call-done = f32[16,384]{1,0:T(8,128)} async-done(((f32[16,6144]{1,0:T(8,128)}), f32[16,384]{1,0:T(8,128)}) %reduce-scatter.24.cloned.1.call-update) | async-done | bytes 24592 | tf_op jit(solution)/shard_map/reduce_scatter | solution.py:99
  1404.5 23.5 %all_gather.18 = f32[16,6144]{1,0:T(8,128)S(1)} all-gather(f32[16,384]{1,0:T(8,128)S(1)} %sub.64), channel_id=1, replica_groups=mesh['vox'=8,'fas'=16] {'fas'}, dimensions={1}, use_global_device_ids=true | all-gather | bytes 417792 | tf_op jit(solution)/shard_map/all_gather | solution.py:104
  1432.6 13.4 fusion.159
  1448.3 57.9 %all-reduce.12.cloned.1.call-done = f32[32768]{0:T(1024)} async-done(((f32[32768]{0:T(1024)}), f32[32768]{0:T(1024)}) %all-reduce.12.cloned.1.call-update) | async-done | bytes 131088 | tf_op jit(solution)/shard_map/psum | solution.py:105
  1508.6 28.1 %while.219 = (s32[]{:T(128)}, f32[16,6144]{1,0:T(8,128)S(1)}, s32[]{:T(128)}, s32[256]{0:T(256)S(1)}, s32[]{:T(128)}, /*index=5*/bf16[256,64,64]{2,1,0:T(8,128)(...) while((s32[]{:T(128)}, f32[16,6144]{1,0:T(8,128)S(1)}, ...), condition=%wide.region_52.53_spmd.clone, body=%wide.region_51.52_spmd.clone.sunk | while | flops 1512153856 | bytes 31263864 | solution.py:68
  1537.6 70.8 %reduce-scatter.26.cloned.1.call-done = f32[16,384]{1,0:T(8,128)} async-done(((f32[16,6144]{1,0:T(8,128)}), f32[16,384]{1,0:T(8,128)}) %reduce-scatter.26.cloned.1.call-update) | async-done | bytes 24592 | tf_op jit(solution)/shard_map/reduce_scatter | solution.py:99
  1609.8 38.8 %psum.115 = f32[]{:T(128)} all-reduce(f32[]{:T(128)} %get-tuple-element.2454), channel_id=1, replica_groups=mesh['vox'=8,'fas'=16] {'fas'}, use_global_device_ids=true, to_apply=%region_50.51 | all-reduce | flops 1 | bytes 8 | tf_op jit(solution)/shard_map/psum | solution.py:109
  1648.6 62.8 %psum.116 = f32[]{:T(128)} all-reduce(f32[]{:T(128)} %multiply_reduce_fusion.6), channel_id=1, replica_groups=mesh['vox'=8,'fas'=16] {'vox','fas'}, use_global_device_ids=true, to_apply=%region_55.56 | all-reduce | flops 1 | bytes 8 | tf_op jit(solution)/shard_map/psum | solution.py:110
  1713.6 28.3 %while.220 = (s32[]{:T(128)}, f32[16,6144]{1,0:T(8,128)S(1)}, s32[]{:T(128)}, s32[256]{0:T(256)S(1)}, s32[]{:T(128)}, /*index=5*/bf16[256,64,64]{2,1,0:T(8,128)(...) while((s32[]{:T(128)}, f32[16,6144]{1,0:T(8,128)S(1)}, ...), condition=%wide.region_57.58_spmd.clone, body=%wide.region_56.57_spmd.clone.sunk | while | flops 1512153856 | bytes 31263864 | solution.py:68
  1742.7 69.0 %reduce-scatter.28.cloned.1.call-done = f32[16,384]{1,0:T(8,128)} async-done(((f32[16,6144]{1,0:T(8,128)}), f32[16,384]{1,0:T(8,128)}) %reduce-scatter.28.cloned.1.call-update) | async-done | bytes 24592 | tf_op jit(solution)/shard_map/reduce_scatter | solution.py:99
  1812.5 23.5 %all_gather.19 = f32[16,6144]{1,0:T(8,128)S(1)} all-gather(f32[16,384]{1,0:T(8,128)S(1)} %sub.66), channel_id=1, replica_groups=mesh['vox'=8,'fas'=16] {'fas'}, dimensions={1}, use_global_device_ids=true | all-gather | bytes 417792 | tf_op jit(solution)/shard_map/all_gather | solution.py:104
  1840.5 13.4 fusion.160
  1856.2 58.0 %all-reduce.14.cloned.1.call-done = f32[32768]{0:T(1024)} async-done(((f32[32768]{0:T(1024)}), f32[32768]{0:T(1024)}) %all-reduce.14.cloned.1.call-update) | async-done | bytes 131088 | tf_op jit(solution)/shard_map/psum | solution.py:105
  1916.6 28.1 %while.222 = (s32[]{:T(128)}, f32[16,6144]{1,0:T(8,128)S(1)}, s32[]{:T(128)}, s32[256]{0:T(256)S(1)}, s32[]{:T(128)}, /*index=5*/bf16[256,64,64]{2,1,0:T(8,128)(...) while((s32[]{:T(128)}, f32[16,6144]{1,0:T(8,128)S(1)}, ...), condition=%wide.region_66.67_spmd.clone, body=%wide.region_65.66_spmd.clone.sunk | while | flops 1512153856 | bytes 31263864 | solution.py:68
  1945.5 70.8 %reduce-scatter.30.cloned.1.call-done = f32[16,384]{1,0:T(8,128)} async-done(((f32[16,6144]{1,0:T(8,128)}), f32[16,384]{1,0:T(8,128)}) %reduce-scatter.30.cloned.1.call-update) | async-done | bytes 24592 | tf_op jit(solution)/shard_map/reduce_scatter | solution.py:99
  2017.8 38.8 %psum.118 = f32[]{:T(128)} all-reduce(f32[]{:T(128)} %get-tuple-element.2452), channel_id=1, replica_groups=mesh['vox'=8,'fas'=16] {'fas'}, use_global_device_ids=true, to_apply=%region_64.65 | all-reduce | flops 1 | bytes 8 | tf_op jit(solution)/shard_map/psum | solution.py:109
  2056.5 62.7 %psum.119 = f32[]{:T(128)} all-reduce(f32[]{:T(128)} %multiply_reduce_fusion.5), channel_id=1, replica_groups=mesh['vox'=8,'fas'=16] {'vox','fas'}, use_global_device_ids=true, to_apply=%region_69.70 | all-reduce | flops 1 | bytes 8 | tf_op jit(solution)/shard_map/psum | solution.py:110
  2121.5 28.2 %while.223 = (s32[]{:T(128)}, f32[16,6144]{1,0:T(8,128)S(1)}, s32[]{:T(128)}, s32[256]{0:T(256)S(1)}, s32[]{:T(128)}, /*index=5*/bf16[256,64,64]{2,1,0:T(8,128)(...) while((s32[]{:T(128)}, f32[16,6144]{1,0:T(8,128)S(1)}, ...), condition=%wide.region_71.72_spmd.clone, body=%wide.region_70.71_spmd.clone.sunk | while | flops 1512153856 | bytes 31263864 | solution.py:68
  2150.5 69.0 %reduce-scatter.32.cloned.1.call-done = f32[16,384]{1,0:T(8,128)} async-done(((f32[16,6144]{1,0:T(8,128)}), f32[16,384]{1,0:T(8,128)}) %reduce-scatter.32.cloned.1.call-update) | async-done | bytes 24592 | tf_op jit(solution)/shard_map/reduce_scatter | solution.py:99
  (217 shorter events, 395.2 us)
Async XLA Ops:
  7.2 10.8 copy-start.15
  7.2 11.1 copy-start.14
  7.2 11.2 copy-start.16
  7.2 11.2 copy-start.11
  7.2 172.5 %reduce-scatter.12.cloned.1.call-start = ((), (), s32[]{:S(2)}) async-start(), calls=%async_computation.11 | async-start | bytes 417792 | tf_op jit(solution)/shard_map/reduce_scatter | solution.py:99
  18.5 58.1 %copy-start.17 = (s32[256]{0:T(256)S(1)}, s32[256]{0:T(256)}, u32[]{:S(2)}) copy-start(s32[256]{0:T(256)} %param.43) | copy-start | bytes 3076
  76.7 103.0 %copy-start.12 = (f32[16,384]{1,0:T(8,128)S(1)}, f32[16,384]{1,0:T(8,128)}, u32[]{:S(2)}) copy-start(f32[16,384]{1,0:T(8,128)} %param.40) | copy-start | bytes 73732
  104.6 0.7 copy-start.1
  105.4 176.9 %all-reduce.6.cloned.1.call-start = ((), (), s32[]{:S(2)}) async-start(), calls=%async_computation.12 | async-start | bytes 262144 | tf_op jit(solution)/shard_map/psum | solution.py:105
  224.2 160.4 %reduce-scatter.14.cloned.1.call-start = ((), (), s32[]{:S(2)}) async-start(), calls=%async_computation.13 | async-start | bytes 417792 | tf_op jit(solution)/shard_map/reduce_scatter | solution.py:99
  313.0 0.7 copy-start.2
  313.8 274.0 %reduce-scatter.16.cloned.1.call-start = ((), (), s32[]{:S(2)}) async-start(), calls=%async_computation.14 | async-start | bytes 417792 | tf_op jit(solution)/shard_map/reduce_scatter | solution.py:99
  517.9 0.7 copy-start.3
  518.7 171.6 %all-reduce.8.cloned.1.call-start = ((), (), s32[]{:S(2)}) async-start(), calls=%async_computation.15 | async-start | bytes 262144 | tf_op jit(solution)/shard_map/psum | solution.py:105
  632.2 160.2 %reduce-scatter.18.cloned.1.call-start = ((), (), s32[]{:S(2)}) async-start(), calls=%async_computation.16 | async-start | bytes 417792 | tf_op jit(solution)/shard_map/reduce_scatter | solution.py:99
  720.8 0.7 copy-start.4
  721.6 274.2 %reduce-scatter.20.cloned.1.call-start = ((), (), s32[]{:S(2)}) async-start(), calls=%async_computation.17 | async-start | bytes 417792 | tf_op jit(solution)/shard_map/reduce_scatter | solution.py:99
  926.0 0.7 copy-start.5
  926.8 171.5 %all-reduce.10.cloned.1.call-start = ((), (), s32[]{:S(2)}) async-start(), calls=%async_computation.18 | async-start | bytes 262144 | tf_op jit(solution)/shard_map/psum | solution.py:105
  1040.2 160.2 %reduce-scatter.22.cloned.1.call-start = ((), (), s32[]{:S(2)}) async-start(), calls=%async_computation.19 | async-start | bytes 417792 | tf_op jit(solution)/shard_map/reduce_scatter | solution.py:99
  1128.8 0.7 copy-start.6
  1129.6 274.2 %reduce-scatter.24.cloned.1.call-start = ((), (), s32[]{:S(2)}) async-start(), calls=%async_computation.20 | async-start | bytes 417792 | tf_op jit(solution)/shard_map/reduce_scatter | solution.py:99
  1333.9 0.7 copy-start.7
  1334.7 171.5 %all-reduce.12.cloned.1.call-start = ((), (), s32[]{:S(2)}) async-start(), calls=%async_computation.21 | async-start | bytes 262144 | tf_op jit(solution)/shard_map/psum | solution.py:105
  1448.2 160.2 %reduce-scatter.26.cloned.1.call-start = ((), (), s32[]{:S(2)}) async-start(), calls=%async_computation.22 | async-start | bytes 417792 | tf_op jit(solution)/shard_map/reduce_scatter | solution.py:99
  1536.8 0.7 copy-start.8
  1537.5 274.2 %reduce-scatter.28.cloned.1.call-start = ((), (), s32[]{:S(2)}) async-start(), calls=%async_computation.23 | async-start | bytes 417792 | tf_op jit(solution)/shard_map/reduce_scatter | solution.py:99
  1741.9 0.7 copy-start.9
  1742.7 171.5 %all-reduce.14.cloned.1.call-start = ((), (), s32[]{:S(2)}) async-start(), calls=%async_computation.24 | async-start | bytes 262144 | tf_op jit(solution)/shard_map/psum | solution.py:105
  1856.1 160.2 %reduce-scatter.30.cloned.1.call-start = ((), (), s32[]{:S(2)}) async-start(), calls=%async_computation.25 | async-start | bytes 417792 | tf_op jit(solution)/shard_map/reduce_scatter | solution.py:99
  1944.7 0.7 copy-start.10
  1945.5 274.0 %reduce-scatter.32.cloned.1.call-start = ((), (), s32[]{:S(2)}) async-start(), calls=%async_computation.26 | async-start | bytes 417792 | tf_op jit(solution)/shard_map/reduce_scatter | solution.py:99
  2120.6 0.9 copy-start.13
  2149.7 0.7 copy-start
Sparse Core Ops, SparseCore 0:
  105.5 74.1 reduce-scatter.11
  224.3 57.9 all-reduce.5
  313.9 70.6 reduce-scatter.13
  518.8 68.9 reduce-scatter.15
  632.3 57.8 all-reduce.7
  721.7 70.6 reduce-scatter.17
  926.9 68.9 reduce-scatter.19
  1040.4 57.8 all-reduce.9
  1129.7 70.6 reduce-scatter.21
  1334.8 68.9 reduce-scatter.23
  1448.3 57.8 all-reduce.11
  1537.7 70.6 reduce-scatter.25
  1742.8 68.9 reduce-scatter.27
  1856.3 57.8 all-reduce.13
  1945.6 70.6 reduce-scatter.29
  2150.6 68.8 reduce-scatter.31
where the time goes:
time: 2240 us; the launch traced here: 2230 us
  waiting for transfers between devices  1060 us (47%)
  blocking collectives  625 us (28%)
  matrix products  275 us (12%)
  local copies, waits for them, and re-layouts  207 us (9%)
  other arithmetic  30.5 us (1%)
  between operations  22.5 us (1%)
    reduce_scatter x11, waiting for transfers between devices, collect(): lax.psum_scatter(partial_value, 'fas', scatter_dimension=1, tiled=True)  773 us
    psum x5, blocking collectives, local(): image_sq = lax.psum(image_local, ('vox', 'fas'))  314 us
    psum x5, waiting for transfers between devices, local(): lax.psum(backward_partial(whole_rows.reshape(vox_rows, BV, DIRS)), 'vox')  290 us
    psum x5, blocking collectives, local(): grad_sq = lax.psum(jnp.sum(projected * projected), 'fas')  194 us
    dot_general x11, matrix products, forward_accumulate(): jnp.einsum('kvj,kjd->kvd', scaled, atom_blk.astype(jnp.float32), precisio...  124 us
    all_gather x5, blocking collectives, local(): whole_rows = lax.all_gather(residual, 'fas', axis=1, tiled=True)  118 us
    dot_general x11, local copies, waits for them, and re-layouts, forward_accumulate(): jnp.einsum('kvj,kjd->kvd', scaled, atom_blk.astype(jnp.float32), precisio...  94.4 us
    dot_general x11, matrix products, forward_accumulate(): jnp.dot(selector.T, image_blk.reshape(group_size, row_width), precision=l...  81.8 us
  transfers between devices with their start and end apart: 16, of which 16 were waited for; matrix products, arithmetic and copies ran while one was open for 0% of the time, Pallas kernels for 0%

commit v1 on v0

--- a/solution.py
+++ b/solution.py
@@ -101,7 +101,26 @@
     weights = initial_weights
     residual = collect(forward_partial(weights)) - signal
     for sweep in range(ITERS):
-        whole_rows = lax.all_gather(residual, "fas", axis=1, tiled=True)
+        peers, position, width = (lax.axis_size("fas"), lax.axis_index("fas"), residual.shape[1])
+        upward = [(i, (i + 1) % peers) for i in range(peers)]
+        left = [(i, (i - 1) % peers) for i in range(peers)]
+        out = jnp.zeros(
+            (*residual.shape[:1], peers * width, *residual.shape[1 + 1 :]), residual.dtype
+        )
+        out = lax.dynamic_update_slice_in_dim(out, residual, position * width, axis=1)
+        from_left = from_right = residual
+        half = peers // 2
+        for step in range(1, half + 1):
+            from_left = lax.ppermute(from_left, "fas", upward)
+            out = lax.dynamic_update_slice_in_dim(
+                out, from_left, (position - step) % peers * width, axis=1
+            )
+            if step < peers - half:
+                from_right = lax.ppermute(from_right, "fas", left)
+                out = lax.dynamic_update_slice_in_dim(
+                    out, from_right, (position + step) % peers * width, axis=1
+                )
+        whole_rows = out
         gradient = lax.psum(backward_partial(whole_rows.reshape(vox_rows, BV, DIRS)), "vox")
         projected = jnp.where((weights > 0) | (gradient < 0), gradient, 0.0)
         image_pred = collect(forward_partial(projected))

time: 2240 us -> 2400 us (1.071)
  starting transfers between devices: 0.65 us -> 190 us
  blocking collectives: 625 us -> 507 us
  waiting for transfers between devices: 1060 us -> 1150 us
    ppermute x0 -> x75, starting transfers between devices: none -> 189 us  [the longest x35 181 us: local(): from_right = lax.ppermute(from_right, 'fas', left)]
    all_gather x5 -> x0, blocking collectives: 118 us -> none  [local(): whole_rows = lax.all_gather(residual, 'fas', axis=1, tiled=True)]
    ppermute x0 -> x75, waiting for transfers between devices: none -> 98.7 us  [the longest x40 98.6 us: local(): from_left = lax.ppermute(from_left, 'fas', upward)]
  transfers between devices with their start and end apart: 16 -> 91, of which waited for: 16 -> 56; matrix products, arithmetic and copies ran while one was open for 0% -> 0% of each run, Pallas kernels for 0% -> 0%
where the time goes in v1:
time: 2400 us; the launch traced here: 2390 us
  waiting for transfers between devices  1150 us (48%)
  blocking collectives  507 us (21%)
  matrix products  276 us (12%)
  local copies, waits for them, and re-layouts  208 us (9%)
  starting transfers between devices  190 us (8%)
  other arithmetic  30.9 us (1%)
    reduce_scatter x11, waiting for transfers between devices, collect(): lax.psum_scatter(partial_value, 'fas', scatter_dimension=1, tiled=True)  773 us
    psum x5, blocking collectives, local(): image_sq = lax.psum(image_local, ('vox', 'fas'))  314 us
    psum x5, waiting for transfers between devices, local(): lax.psum(backward_partial(whole_rows.reshape(vox_rows, BV, DIRS)), 'vox')  278 us
    psum x5, blocking collectives, local(): grad_sq = lax.psum(jnp.sum(projected * projected), 'fas')  194 us
    ppermute x35, starting transfers between devices, local(): from_right = lax.ppermute(from_right, 'fas', left)  181 us
    dot_general x11, matrix products, forward_accumulate(): jnp.einsum('kvj,kjd->kvd', scaled, atom_blk.astype(jnp.float32), precisio...  124 us
    ppermute x40, waiting for transfers between devices, local(): from_left = lax.ppermute(from_left, 'fas', upward)  98.6 us
    dot_general x11, local copies, waits for them, and re-layouts, forward_accumulate(): jnp.einsum('kvj,kjd->kvd', scaled, atom_blk.astype(jnp.float32), precisio...  94.1 us
  transfers between devices with their start and end apart: 91, of which 56 were waited for; matrix products, arithmetic and copies ran while one was open for 0% of the time, Pallas kernels for 0%

profile of v1, /device:TPU:0, one launch (start us, length us, event | category | flops | bytes accessed | tf_op | source)
XLA Modules:
  0.0 2387.6 jit_solution(17469126836601933745)
XLA Ops:
  20.8 57.4 %gather_fusion = bf16[16384,96]{1,0:T(8,128)(2,1)} fusion(bf16[360,96]{1,0:T(8,128)(2,1)S(1)} %copy.28, s32[16384]{0:T(1024)S(1)} %broadcast_clamp_fusion), kind=kCustom, calls=%fused_computation | custom fusion | bytes 6356992 | tf_op jit(solution)/shard_map/gather | solution.py:30
  78.2 28.0 %while.208 = (s32[]{:T(128)}, f32[16,6144]{1,0:T(8,128)S(1)}, s32[]{:T(128)}, s32[256]{0:T(256)S(1)}, s32[]{:T(128)}, /*index=5*/bf16[256,64,64]{2,1,0:T(8,128)(...) while((s32[]{:T(128)}, f32[16,6144]{1,0:T(8,128)S(1)}, ...), condition=%wide.region_1.2_spmd.clone, body=%wide.region_0.1_spmd.clone.sunk | while | flops 1512153856 | bytes 31263864 | solution.py:68
  107.0 74.3 %reduce-scatter.12.cloned.1.call-done = f32[16,384]{1,0:T(8,128)} async-done(((f32[16,6144]{1,0:T(8,128)}), f32[16,384]{1,0:T(8,128)}) %reduce-scatter.12.cloned.1.call-update) | async-done | bytes 24592 | tf_op jit(solution)/shard_map/reduce_scatter | solution.py:99
  244.7 13.5 fusion.156
  260.4 55.6 %all-reduce.6.cloned.1.call-done = f32[32768]{0:T(1024)} async-done(((f32[32768]{0:T(1024)}), f32[32768]{0:T(1024)}) %all-reduce.6.cloned.1.call-update) | async-done | bytes 131088 | tf_op jit(solution)/shard_map/psum | solution.py:124
  318.4 28.1 %while.210 = (s32[]{:T(128)}, f32[16,6144]{1,0:T(8,128)S(1)}, s32[]{:T(128)}, s32[256]{0:T(256)S(1)}, s32[]{:T(128)}, /*index=5*/bf16[256,64,64]{2,1,0:T(8,128)(...) while((s32[]{:T(128)}, f32[16,6144]{1,0:T(8,128)S(1)}, ...), condition=%wide.region_10.11_spmd.clone, body=%wide.region_9.10_spmd.clone.sunk | while | flops 1512153856 | bytes 31263864 | solution.py:68
  347.4 70.8 %reduce-scatter.14.cloned.1.call-done = f32[16,384]{1,0:T(8,128)} async-done(((f32[16,6144]{1,0:T(8,128)}), f32[16,384]{1,0:T(8,128)}) %reduce-scatter.14.cloned.1.call-update) | async-done | bytes 24592 | tf_op jit(solution)/shard_map/reduce_scatter | solution.py:99
  419.5 38.8 %psum.106 = f32[]{:T(128)} all-reduce(f32[]{:T(128)} %get-tuple-element.2468), channel_id=1, replica_groups=mesh['vox'=8,'fas'=16] {'fas'}, use_global_device_ids=true, to_apply=%region_8.9 | all-reduce | flops 1 | bytes 8 | tf_op jit(solution)/shard_map/psum | solution.py:128
  458.3 62.7 %psum.107 = f32[]{:T(128)} all-reduce(f32[]{:T(128)} %multiply_reduce_fusion.9), channel_id=1, replica_groups=mesh['vox'=8,'fas'=16] {'vox','fas'}, use_global_device_ids=true, to_apply=%region_13.14 | all-reduce | flops 1 | bytes 8 | tf_op jit(solution)/shard_map/psum | solution.py:129
  523.2 28.2 %while.211 = (s32[]{:T(128)}, f32[16,6144]{1,0:T(8,128)S(1)}, s32[]{:T(128)}, s32[256]{0:T(256)S(1)}, s32[]{:T(128)}, /*index=5*/bf16[256,64,64]{2,1,0:T(8,128)(...) while((s32[]{:T(128)}, f32[16,6144]{1,0:T(8,128)S(1)}, ...), condition=%wide.region_15.16_spmd.clone, body=%wide.region_14.15_spmd.clone.sunk | while | flops 1512153856 | bytes 31263864 | solution.py:68
  523.4 11.3 fusion.279
  552.2 69.1 %reduce-scatter.16.cloned.1.call-done = f32[16,384]{1,0:T(8,128)} async-done(((f32[16,6144]{1,0:T(8,128)}), f32[16,384]{1,0:T(8,128)}) %reduce-scatter.16.cloned.1.call-update) | async-done | bytes 24592 | tf_op jit(solution)/shard_map/reduce_scatter | solution.py:99
  684.2 13.4 fusion.157
  699.9 55.7 %all-reduce.8.cloned.1.call-done = f32[32768]{0:T(1024)} async-done(((f32[32768]{0:T(1024)}), f32[32768]{0:T(1024)}) %all-reduce.8.cloned.1.call-update) | async-done | bytes 131088 | tf_op jit(solution)/shard_map/psum | solution.py:124
  758.0 28.1 %while.213 = (s32[]{:T(128)}, f32[16,6144]{1,0:T(8,128)S(1)}, s32[]{:T(128)}, s32[256]{0:T(256)S(1)}, s32[]{:T(128)}, /*index=5*/bf16[256,64,64]{2,1,0:T(8,128)(...) while((s32[]{:T(128)}, f32[16,6144]{1,0:T(8,128)S(1)}, ...), condition=%wide.region_24.25_spmd.clone, body=%wide.region_23.24_spmd.clone.sunk | while | flops 1512153856 | bytes 31263864 | solution.py:68
  758.2 11.3 fusion.286
  786.9 70.8 %reduce-scatter.18.cloned.1.call-done = f32[16,384]{1,0:T(8,128)} async-done(((f32[16,6144]{1,0:T(8,128)}), f32[16,384]{1,0:T(8,128)}) %reduce-scatter.18.cloned.1.call-update) | async-done | bytes 24592 | tf_op jit(solution)/shard_map/reduce_scatter | solution.py:99
  859.1 38.8 %psum.109 = f32[]{:T(128)} all-reduce(f32[]{:T(128)} %get-tuple-element.2464), channel_id=1, replica_groups=mesh['vox'=8,'fas'=16] {'fas'}, use_global_device_ids=true, to_apply=%region_22.23 | all-reduce | flops 1 | bytes 8 | tf_op jit(solution)/shard_map/psum | solution.py:128
  897.9 62.7 %psum.110 = f32[]{:T(128)} all-reduce(f32[]{:T(128)} %multiply_reduce_fusion.8), channel_id=1, replica_groups=mesh['vox'=8,'fas'=16] {'vox','fas'}, use_global_device_ids=true, to_apply=%region_27.28 | all-reduce | flops 1 | bytes 8 | tf_op jit(solution)/shard_map/psum | solution.py:129
  962.8 28.2 %while.214 = (s32[]{:T(128)}, f32[16,6144]{1,0:T(8,128)S(1)}, s32[]{:T(128)}, s32[256]{0:T(256)S(1)}, s32[]{:T(128)}, /*index=5*/bf16[256,64,64]{2,1,0:T(8,128)(...) while((s32[]{:T(128)}, f32[16,6144]{1,0:T(8,128)S(1)}, ...), condition=%wide.region_29.30_spmd.clone, body=%wide.region_28.29_spmd.clone.sunk | while | flops 1512153856 | bytes 31263864 | solution.py:68
  963.0 11.3 fusion.291
  991.8 69.0 %reduce-scatter.20.cloned.1.call-done = f32[16,384]{1,0:T(8,128)} async-done(((f32[16,6144]{1,0:T(8,128)}), f32[16,384]{1,0:T(8,128)}) %reduce-scatter.20.cloned.1.call-update) | async-done | bytes 24592 | tf_op jit(solution)/shard_map/reduce_scatter | solution.py:99
  1123.8 13.4 fusion.158
  1139.5 55.6 %all-reduce.10.cloned.1.call-done = f32[32768]{0:T(1024)} async-done(((f32[32768]{0:T(1024)}), f32[32768]{0:T(1024)}) %all-reduce.10.cloned.1.call-update) | async-done | bytes 131088 | tf_op jit(solution)/shard_map/psum | solution.py:124
  1197.6 28.1 %while.216 = (s32[]{:T(128)}, f32[16,6144]{1,0:T(8,128)S(1)}, s32[]{:T(128)}, s32[256]{0:T(256)S(1)}, s32[]{:T(128)}, /*index=5*/bf16[256,64,64]{2,1,0:T(8,128)(...) while((s32[]{:T(128)}, f32[16,6144]{1,0:T(8,128)S(1)}, ...), condition=%wide.region_38.39_spmd.clone, body=%wide.region_37.38_spmd.clone.sunk | while | flops 1512153856 | bytes 31263864 | solution.py:68
  1197.8 11.3 fusion.298
  1226.5 70.8 %reduce-scatter.22.cloned.1.call-done = f32[16,384]{1,0:T(8,128)} async-done(((f32[16,6144]{1,0:T(8,128)}), f32[16,384]{1,0:T(8,128)}) %reduce-scatter.22.cloned.1.call-update) | async-done | bytes 24592 | tf_op jit(solution)/shard_map/reduce_scatter | solution.py:99
  1298.7 38.8 %psum.112 = f32[]{:T(128)} all-reduce(f32[]{:T(128)} %get-tuple-element.2460), channel_id=1, replica_groups=mesh['vox'=8,'fas'=16] {'fas'}, use_global_device_ids=true, to_apply=%region_36.37 | all-reduce | flops 1 | bytes 8 | tf_op jit(solution)/shard_map/psum | solution.py:128
  1337.5 62.7 %psum.113 = f32[]{:T(128)} all-reduce(f32[]{:T(128)} %multiply_reduce_fusion.7), channel_id=1, replica_groups=mesh['vox'=8,'fas'=16] {'vox','fas'}, use_global_device_ids=true, to_apply=%region_41.42 | all-reduce | flops 1 | bytes 8 | tf_op jit(solution)/shard_map/psum | solution.py:129
  1402.3 28.2 %while.217 = (s32[]{:T(128)}, f32[16,6144]{1,0:T(8,128)S(1)}, s32[]{:T(128)}, s32[256]{0:T(256)S(1)}, s32[]{:T(128)}, /*index=5*/bf16[256,64,64]{2,1,0:T(8,128)(...) while((s32[]{:T(128)}, f32[16,6144]{1,0:T(8,128)S(1)}, ...), condition=%wide.region_43.44_spmd.clone, body=%wide.region_42.43_spmd.clone.sunk | while | flops 1512153856 | bytes 31263864 | solution.py:68
  1431.3 69.0 %reduce-scatter.24.cloned.1.call-done = f32[16,384]{1,0:T(8,128)} async-done(((f32[16,6144]{1,0:T(8,128)}), f32[16,384]{1,0:T(8,128)}) %reduce-scatter.24.cloned.1.call-update) | async-done | bytes 24592 | tf_op jit(solution)/shard_map/reduce_scatter | solution.py:99
  1563.4 13.4 fusion.159
  1579.1 55.7 %all-reduce.12.cloned.1.call-done = f32[32768]{0:T(1024)} async-done(((f32[32768]{0:T(1024)}), f32[32768]{0:T(1024)}) %all-reduce.12.cloned.1.call-update) | async-done | bytes 131088 | tf_op jit(solution)/shard_map/psum | solution.py:124
  1637.1 28.1 %while.219 = (s32[]{:T(128)}, f32[16,6144]{1,0:T(8,128)S(1)}, s32[]{:T(128)}, s32[256]{0:T(256)S(1)}, s32[]{:T(128)}, /*index=5*/bf16[256,64,64]{2,1,0:T(8,128)(...) while((s32[]{:T(128)}, f32[16,6144]{1,0:T(8,128)S(1)}, ...), condition=%wide.region_52.53_spmd.clone, body=%wide.region_51.52_spmd.clone.sunk | while | flops 1512153856 | bytes 31263864 | solution.py:68
  1637.3 11.3 fusion.310
  1666.1 70.8 %reduce-scatter.26.cloned.1.call-done = f32[16,384]{1,0:T(8,128)} async-done(((f32[16,6144]{1,0:T(8,128)}), f32[16,384]{1,0:T(8,128)}) %reduce-scatter.26.cloned.1.call-update) | async-done | bytes 24592 | tf_op jit(solution)/shard_map/reduce_scatter | solution.py:99
  1738.3 38.8 %psum.115 = f32[]{:T(128)} all-reduce(f32[]{:T(128)} %get-tuple-element.2456), channel_id=1, replica_groups=mesh['vox'=8,'fas'=16] {'fas'}, use_global_device_ids=true, to_apply=%region_50.51 | all-reduce | flops 1 | bytes 8 | tf_op jit(solution)/shard_map/psum | solution.py:128
  1777.0 62.7 %psum.116 = f32[]{:T(128)} all-reduce(f32[]{:T(128)} %multiply_reduce_fusion.6), channel_id=1, replica_groups=mesh['vox'=8,'fas'=16] {'vox','fas'}, use_global_device_ids=true, to_apply=%region_55.56 | all-reduce | flops 1 | bytes 8 | tf_op jit(solution)/shard_map/psum | solution.py:129
  1841.9 28.2 %while.220 = (s32[]{:T(128)}, f32[16,6144]{1,0:T(8,128)S(1)}, s32[]{:T(128)}, s32[256]{0:T(256)S(1)}, s32[]{:T(128)}, /*index=5*/bf16[256,64,64]{2,1,0:T(8,128)(...) while((s32[]{:T(128)}, f32[16,6144]{1,0:T(8,128)S(1)}, ...), condition=%wide.region_57.58_spmd.clone, body=%wide.region_56.57_spmd.clone.sunk | while | flops 1512153856 | bytes 31263864 | solution.py:68
  1870.9 69.0 %reduce-scatter.28.cloned.1.call-done = f32[16,384]{1,0:T(8,128)} async-done(((f32[16,6144]{1,0:T(8,128)}), f32[16,384]{1,0:T(8,128)}) %reduce-scatter.28.cloned.1.call-update) | async-done | bytes 24592 | tf_op jit(solution)/shard_map/reduce_scatter | solution.py:99
  2002.9 13.4 fusion.160
  2018.6 55.7 %all-reduce.14.cloned.1.call-done = f32[32768]{0:T(1024)} async-done(((f32[32768]{0:T(1024)}), f32[32768]{0:T(1024)}) %all-reduce.14.cloned.1.call-update) | async-done | bytes 131088 | tf_op jit(solution)/shard_map/psum | solution.py:124
  2076.7 28.1 %while.222 = (s32[]{:T(128)}, f32[16,6144]{1,0:T(8,128)S(1)}, s32[]{:T(128)}, s32[256]{0:T(256)S(1)}, s32[]{:T(128)}, /*index=5*/bf16[256,64,64]{2,1,0:T(8,128)(...) while((s32[]{:T(128)}, f32[16,6144]{1,0:T(8,128)S(1)}, ...), condition=%wide.region_66.67_spmd.clone, body=%wide.region_65.66_spmd.clone.sunk | while | flops 1512153856 | bytes 31263864 | solution.py:68
  2105.7 70.8 %reduce-scatter.30.cloned.1.call-done = f32[16,384]{1,0:T(8,128)} async-done(((f32[16,6144]{1,0:T(8,128)}), f32[16,384]{1,0:T(8,128)}) %reduce-scatter.30.cloned.1.call-update) | async-done | bytes 24592 | tf_op jit(solution)/shard_map/reduce_scatter | solution.py:99
  2177.8 38.8 %psum.118 = f32[]{:T(128)} all-reduce(f32[]{:T(128)} %get-tuple-element.2452), channel_id=1, replica_groups=mesh['vox'=8,'fas'=16] {'fas'}, use_global_device_ids=true, to_apply=%region_64.65 | all-reduce | flops 1 | bytes 8 | tf_op jit(solution)/shard_map/psum | solution.py:128
  2216.6 62.7 %psum.119 = f32[]{:T(128)} all-reduce(f32[]{:T(128)} %multiply_reduce_fusion.5), channel_id=1, replica_groups=mesh['vox'=8,'fas'=16] {'vox','fas'}, use_global_device_ids=true, to_apply=%region_69.70 | all-reduce | flops 1 | bytes 8 | tf_op jit(solution)/shard_map/psum | solution.py:129
  2281.5 28.2 %while.223 = (s32[]{:T(128)}, f32[16,6144]{1,0:T(8,128)S(1)}, s32[]{:T(128)}, s32[256]{0:T(256)S(1)}, s32[]{:T(128)}, /*index=5*/bf16[256,64,64]{2,1,0:T(8,128)(...) while((s32[]{:T(128)}, f32[16,6144]{1,0:T(8,128)S(1)}, ...), condition=%wide.region_71.72_spmd.clone, body=%wide.region_70.71_spmd.clone.sunk | while | flops 1512153856 | bytes 31263864 | solution.py:68
  2310.4 69.1 %reduce-scatter.32.cloned.1.call-done = f32[16,384]{1,0:T(8,128)} async-done(((f32[16,6144]{1,0:T(8,128)}), f32[16,384]{1,0:T(8,128)}) %reduce-scatter.32.cloned.1.call-update) | async-done | bytes 24592 | tf_op jit(solution)/shard_map/reduce_scatter | solution.py:99
  (437 shorter events, 629.1 us)
Async XLA Ops:
  7.2 174.0 %reduce-scatter.12.cloned.1.call-start = ((), (), s32[]{:S(2)}) async-start(), calls=%async_computation.11 | async-start | bytes 417792 | tf_op jit(solution)/shard_map/reduce_scatter | solution.py:99
  106.9 209.1 %all-reduce.6.cloned.1.call-start = ((), (), s32[]{:S(2)}) async-start(), calls=%async_computation.12 | async-start | bytes 262144 | tf_op jit(solution)/shard_map/psum | solution.py:124
  182.0 7.1 collective-permute-start
  189.2 7.4 collective-permute-start.2
  196.6 7.1 collective-permute-start.4
  196.6 7.1 collective-permute-start.5
  203.7 7.2 collective-permute-start.6
  203.7 7.2 collective-permute-start.7
  211.0 7.1 collective-permute-start.8
  211.0 7.1 collective-permute-start.9
  218.1 7.1 collective-permute-start.10
  218.1 7.1 collective-permute-start.11
  225.3 7.1 collective-permute-start.12
  225.3 7.7 collective-permute-start.13
  232.4 7.7 collective-permute-start.14
  260.3 157.8 %reduce-scatter.14.cloned.1.call-start = ((), (), s32[]{:S(2)}) async-start(), calls=%async_computation.13 | async-start | bytes 417792 | tf_op jit(solution)/shard_map/reduce_scatter | solution.py:99
  347.3 273.9 %reduce-scatter.16.cloned.1.call-start = ((), (), s32[]{:S(2)}) async-start(), calls=%async_computation.14 | async-start | bytes 417792 | tf_op jit(solution)/shard_map/reduce_scatter | solution.py:99
  552.1 203.5 %all-reduce.8.cloned.1.call-start = ((), (), s32[]{:S(2)}) async-start(), calls=%async_computation.15 | async-start | bytes 262144 | tf_op jit(solution)/shard_map/psum | solution.py:124
  643.4 7.2 collective-permute-start.21
  643.5 7.2 collective-permute-start.22
  650.7 7.6 collective-permute-start.24
  657.8 7.5 collective-permute-start.25
  665.3 7.1 collective-permute-start.27
  699.9 157.9 %reduce-scatter.18.cloned.1.call-start = ((), (), s32[]{:S(2)}) async-start(), calls=%async_computation.16 | async-start | bytes 417792 | tf_op jit(solution)/shard_map/reduce_scatter | solution.py:99
  786.9 273.9 %reduce-scatter.20.cloned.1.call-start = ((), (), s32[]{:S(2)}) async-start(), calls=%async_computation.17 | async-start | bytes 417792 | tf_op jit(solution)/shard_map/reduce_scatter | solution.py:99
  991.7 203.4 %all-reduce.10.cloned.1.call-start = ((), (), s32[]{:S(2)}) async-start(), calls=%async_computation.18 | async-start | bytes 262144 | tf_op jit(solution)/shard_map/psum | solution.py:124
  1083.0 7.2 collective-permute-start.36
  1083.0 7.2 collective-permute-start.37
  1090.3 7.6 collective-permute-start.39
  1097.4 7.5 collective-permute-start.40
  1139.5 157.8 %reduce-scatter.22.cloned.1.call-start = ((), (), s32[]{:S(2)}) async-start(), calls=%async_computation.19 | async-start | bytes 417792 | tf_op jit(solution)/shard_map/reduce_scatter | solution.py:99
  1226.5 273.9 %reduce-scatter.24.cloned.1.call-start = ((), (), s32[]{:S(2)}) async-start(), calls=%async_computation.20 | async-start | bytes 417792 | tf_op jit(solution)/shard_map/reduce_scatter | solution.py:99
  1431.3 203.5 %all-reduce.12.cloned.1.call-start = ((), (), s32[]{:S(2)}) async-start(), calls=%async_computation.21 | async-start | bytes 262144 | tf_op jit(solution)/shard_map/psum | solution.py:124
  1515.4 7.1 collective-permute-start.49
  1522.6 7.2 collective-permute-start.51
  1522.6 7.2 collective-permute-start.52
  1529.8 7.6 collective-permute-start.54
  1536.9 7.5 collective-permute-start.55
  1579.0 157.9 %reduce-scatter.26.cloned.1.call-start = ((), (), s32[]{:S(2)}) async-start(), calls=%async_computation.22 | async-start | bytes 417792 | tf_op jit(solution)/shard_map/reduce_scatter | solution.py:99
  1666.0 273.9 %reduce-scatter.28.cloned.1.call-start = ((), (), s32[]{:S(2)}) async-start(), calls=%async_computation.23 | async-start | bytes 417792 | tf_op jit(solution)/shard_map/reduce_scatter | solution.py:99
  1870.9 203.4 %all-reduce.14.cloned.1.call-start = ((), (), s32[]{:S(2)}) async-start(), calls=%async_computation.24 | async-start | bytes 262144 | tf_op jit(solution)/shard_map/psum | solution.py:124
  1955.0 7.1 collective-permute-start.64
  1962.1 7.2 collective-permute-start.66
  1962.1 7.2 collective-permute-start.67
  1969.4 7.6 collective-permute-start.69
  1976.5 7.5 collective-permute-start.70
  2018.6 157.9 %reduce-scatter.30.cloned.1.call-start = ((), (), s32[]{:S(2)}) async-start(), calls=%async_computation.25 | async-start | bytes 417792 | tf_op jit(solution)/shard_map/reduce_scatter | solution.py:99
  2105.6 273.9 %reduce-scatter.32.cloned.1.call-start = ((), (), s32[]{:S(2)}) async-start(), calls=%async_computation.26 | async-start | bytes 417792 | tf_op jit(solution)/shard_map/reduce_scatter | solution.py:99
  (59 other events, 510.3 us)
Sparse Core Ops, SparseCore 0:
  107.0 74.1 reduce-scatter.11
  260.4 55.5 all-reduce.5
  347.4 70.6 reduce-scatter.13
  552.2 68.9 reduce-scatter.15
  700.0 55.5 all-reduce.7
  787.0 70.6 reduce-scatter.17
  991.8 68.9 reduce-scatter.19
  1139.6 55.5 all-reduce.9
  1226.6 70.6 reduce-scatter.21
  1431.4 68.9 reduce-scatter.23
  1579.1 55.5 all-reduce.11
  1666.2 70.6 reduce-scatter.25
  1871.0 68.8 reduce-scatter.27
  2018.7 55.5 all-reduce.13
  2105.7 70.6 reduce-scatter.29
  2310.6 68.9 reduce-scatter.31
